TPU v7x, 32 devices: a whole 2x2x4 slice. The times are simulated.
32 devices in a mesh: asset: 8 (over z, core), frame: 2 (over y), row: 2 (over x).
Axes of the slice: x: 2, y: 2, z: 4, core: 2. Of those that a mesh axis runs over, the one named last changes fastest.
Arguments:
- latent: bfloat16 [16, 4, 72, 1280], P(('asset', 'frame'), 'row'), parts along dimension 0, may hold values from -36 to 36
- timestep: int32 [8], P('asset'), parts along dimension 0, may hold values from 0 to 999
- camera: int32 [16, 2], P('asset'), parts along dimension 0, may hold values from 0 to 359
- dec_feat: bfloat16 [16, 4, 72, 512], P(('asset', 'frame'), 'row'), parts along dimension 0, may hold values from -36 to 36
- norm_gain: float32 [1280], replicated, may hold values from 0.1 to 1.9
- norm_shift: float32 [1280], replicated, may hold values from -3 to 3
- emb_weight: bfloat16 [960, 1280], replicated, may hold values from -0.375 to 0.375
- conv_weight: bfloat16 [3, 3, 1280, 1280], P(None, None, None, 'frame'), may hold values from -0.0546875 to 0.0546875
- ln_gain: float32 [1280], replicated, may hold values from 0.1 to 1.9
- q_weight: bfloat16 [1280, 1280], P(('frame', 'row')), may hold values from -0.15625 to 0.15625
- k_weight: bfloat16 [1280, 1280], P(('frame', 'row')), may hold values from -0.15625 to 0.15625
- v_weight: bfloat16 [1280, 1280], P(('frame', 'row')), may hold values from -0.15625 to 0.15625
- o_weight: bfloat16 [1280, 1280], P(('frame', 'row')), may hold values from -0.15625 to 0.15625
- dec_gain: float32 [512], replicated, may hold values from 0.1 to 1.9
- dec_shift: float32 [512], replicated, may hold values from -3 to 3
- time_weight: bfloat16 [3, 512, 512], replicated, may hold values from -0.15625 to 0.15625
Outputs:
- unet_out: bfloat16 [16, 4, 72, 1280], P(('asset', 'frame'), 'row'), parts along dimension 0
- dec_out: bfloat16 [16, 4, 72, 512], P(('asset', 'frame'), 'row'), parts along dimension 0
There are 8 independent parts, one for each index of `asset`. A program takes and returns all parts, laid end to end along the dimension named above; an argument that names none is the same for every part. Nothing has to cross between parts.
All inputs are finite; a program needn't handle non-finite values.
Results may differ from a plain program's by a relative error of at most 0.0056.
Values may be sent and summed in bfloat16 or wider, within the bound.
A program may use at most 128 MiB of HBM per device.

v0:
```python
import math

import jax
import jax.numpy as jnp
from jax import lax
from jax.sharding import PartitionSpec as P

HEADS = 20
G = 32


EPSILON = 1e-05


def extended(cells, sides, width):
    for axis, dim in sides:
        count = lax.axis_size(axis)
        ends = count - 1
        head = lax.slice_in_dim(cells, 0, width, axis=dim)
        tail = lax.slice_in_dim(cells, cells.shape[dim] - width, cells.shape[dim], axis=dim)
        cells = jnp.concatenate(
            [
                lax.ppermute(tail, axis, [(i, (i + 1) % count) for i in range(ends)]),
                cells,
                lax.ppermute(head, axis, [((i + 1) % count, i) for i in range(ends)]),
            ],
            axis=dim,
        )
    return cells


def from_behind(block, axis, distance):
    devices = range(lax.axis_size(axis))
    route = [((i - distance) % len(devices), i) for i in devices]
    return lax.ppermute(block, axis, route)


def sinusoids(values, entries):
    half = entries // 2
    freqs = jnp.exp(-math.log(10000.0) * jnp.arange(half, dtype=jnp.float32) / half)
    angles = values.astype(jnp.float32)[..., None] * freqs
    return jnp.concatenate([jnp.cos(angles), jnp.sin(angles)], axis=-1)


def conditions(timestep, camera, frames, entries):
    times = jnp.broadcast_to(timestep.astype(jnp.float32), (frames,))
    pieces = [
        sinusoids(times, entries),
        sinusoids(camera[:, 0], entries),
        sinusoids(camera[:, 1], entries),
    ]
    return jax.nn.silu(jnp.concatenate(pieces, axis=-1)).astype(jnp.bfloat16)


def convolve(kernel, piece):
    number, rimmed, width, channels = piece.shape
    band = rimmed - 2
    outputs = kernel.shape[3]
    widened = jnp.pad(piece, ((0, 0), (0, 0), (1, 1), (0, 0)))
    total = jnp.zeros((number * band * width, outputs), jnp.float32)
    for down in range(3):
        for side in range(3):
            window = widened[:, down : down + band, side : side + width, :].reshape(-1, channels)
            total = total + jnp.dot(window, kernel[down, side], preferred_element_type=jnp.float32)
    return total.reshape(number, band, width, outputs)


def body(
    latent,
    timestep,
    camera,
    dec_feat,
    norm_gain,
    norm_shift,
    emb_weight,
    conv_weight,
    ln_gain,
    q_weight,
    k_weight,
    v_weight,
    o_weight,
    dec_gain,
    dec_shift,
    time_weight,
):
    frame_count = lax.axis_size("frame")
    row_count = lax.axis_size("row")
    frame_index = lax.axis_index("frame")
    local_frames, band, width, channels = latent.shape
    share = conv_weight.shape[3]
    frames = local_frames * frame_count
    groups = G
    heads = HEADS
    head_size = channels // heads
    features = conditions(timestep, camera, frames, emb_weight.shape[0] // 3)
    share_start = frame_index * share
    emb_share = lax.dynamic_slice_in_dim(emb_weight, share_start, share, 1)
    cond_share = jnp.dot(features, emb_share, preferred_element_type=jnp.float32)
    values = latent.astype(jnp.float32)
    grouped = values.reshape(local_frames, band, width, groups, channels // groups)
    sums, squares = lax.psum(
        (jnp.sum(grouped, axis=(1, 2, 4)), jnp.sum(grouped * grouped, axis=(1, 2, 4))), "row"
    )
    number = band * row_count * width * (channels // groups)
    means = sums / number
    scales = lax.rsqrt(squares / number - means * means + EPSILON)
    normed = (grouped - means[:, None, None, :, None]) * scales[:, None, None, :, None]
    normed = normed.reshape(local_frames, band, width, channels) * norm_gain + norm_shift
    act = jax.nn.silu(normed).astype(jnp.bfloat16)
    residual = lax.all_to_all(latent, "frame", split_axis=3, concat_axis=0, tiled=True).astype(
        jnp.float32
    )
    rimmed = extended(act, (("row", 1),), 1)
    conv = convolve(conv_weight, lax.all_gather(rimmed, "frame", axis=0, tiled=True))
    spatial = (residual + conv + cond_share[:, None, None, :]).astype(jnp.bfloat16)
    columns = lax.all_to_all(
        spatial.reshape(frames, band * width, share),
        "frame",
        split_axis=1,
        concat_axis=2,
        tiled=True,
    )
    pixels = columns.shape[1]
    tokens = columns.astype(jnp.float32)
    token_mean = jnp.mean(tokens, axis=-1, keepdims=True)
    token_square = jnp.mean(tokens * tokens, axis=-1, keepdims=True)
    token_scale = lax.rsqrt(token_square - token_mean * token_mean + EPSILON)
    normal = (
        ((tokens - token_mean) * token_scale * ln_gain).astype(jnp.bfloat16).reshape(-1, channels)
    )
    pieces = (
        lax.all_gather(q_weight, ("frame", "row"), axis=0, tiled=True),
        lax.all_gather(k_weight, ("frame", "row"), axis=0, tiled=True),
        lax.all_gather(v_weight, ("frame", "row"), axis=0, tiled=True),
    )
    inputs = normal
    query_rows, key_rows, value_rows = tuple(
        (jnp.dot(inputs, weight_part, preferred_element_type=jnp.float32) for weight_part in pieces)
    )
    query_rows = query_rows.astype(jnp.bfloat16).reshape(frames, pixels, heads, head_size)
    key_rows = key_rows.astype(jnp.bfloat16).reshape(frames, pixels, heads, head_size)
    value_rows = value_rows.astype(jnp.bfloat16).reshape(frames, pixels, heads, head_size)
    scores = jnp.einsum(
        "fphd,gphd->phfg", query_rows, key_rows, preferred_element_type=jnp.float32
    ) * (1.0 / math.sqrt(head_size))
    weights = jnp.exp(scores)
    probs = (weights / jnp.sum(weights, axis=-1, keepdims=True)).astype(jnp.bfloat16)
    mixed = (
        jnp.einsum("phfg,gphd->fphd", probs, value_rows, preferred_element_type=jnp.float32)
        .astype(jnp.bfloat16)
        .reshape(-1, channels)
    )
    inputs = mixed
    attended = jnp.dot(
        inputs,
        lax.all_gather(o_weight, ("frame", "row"), axis=0, tiled=True),
        preferred_element_type=jnp.float32,
    )
    result = (
        (tokens.reshape(-1, channels) + attended)
        .astype(jnp.bfloat16)
        .reshape(frames, pixels, channels)
    )
    unet_out = lax.all_to_all(result, "frame", split_axis=0, concat_axis=1, tiled=True).reshape(
        local_frames, band, width, channels
    )
    dec_frames, dec_band, dec_width, dec_channels = dec_feat.shape
    dec_values = dec_feat.astype(jnp.float32)
    dec_grouped = dec_values.reshape(
        dec_frames, dec_band, dec_width, groups, dec_channels // groups
    )
    dec_sums, dec_squares = lax.psum(
        (
            jnp.sum(dec_grouped, axis=(0, 1, 2, 4)),
            jnp.sum(dec_grouped * dec_grouped, axis=(0, 1, 2, 4)),
        ),
        ("frame", "row"),
    )
    dec_number = (
        dec_frames * frame_count * dec_band * row_count * dec_width * (dec_channels // groups)
    )
    dec_means = dec_sums / dec_number
    dec_scales = lax.rsqrt(dec_squares / dec_number - dec_means * dec_means + EPSILON)
    dec_normed = ((dec_grouped - dec_means[:, None]) * dec_scales[:, None]).reshape(
        dec_frames, dec_band, dec_width, dec_channels
    )
    dec_act = jax.nn.silu(dec_normed * dec_gain + dec_shift).astype(jnp.bfloat16)
    earlier = from_behind(dec_act, "frame", 1)
    later = from_behind(dec_act, "frame", -1)
    before = jnp.concatenate([earlier, dec_act[:-1]], axis=0).reshape(-1, dec_channels)
    after = jnp.concatenate([dec_act[1:], later], axis=0).reshape(-1, dec_channels)
    middle = dec_act.reshape(-1, dec_channels)
    temporal = jnp.dot(before, time_weight[0], preferred_element_type=jnp.float32)
    temporal = temporal + jnp.dot(middle, time_weight[1], preferred_element_type=jnp.float32)
    temporal = temporal + jnp.dot(after, time_weight[2], preferred_element_type=jnp.float32)
    dec_out = (dec_values + temporal.reshape(dec_frames, dec_band, dec_width, dec_channels)).astype(
        jnp.bfloat16
    )
    return (unet_out, dec_out)


def solution(mesh):
    in_specs = (
        P(("asset", "frame"), "row", None, None),
        P("asset"),
        P("asset", None),
        P(("asset", "frame"), "row", None, None),
        P(),
        P(),
        P(),
        P(None, None, None, "frame"),
        P(),
        P(("frame", "row"), None),
        P(("frame", "row"), None),
        P(("frame", "row"), None),
        P(("frame", "row"), None),
        P(),
        P(),
        P(),
    )
    out_specs = (P(("asset", "frame"), "row", None, None), P(("asset", "frame"), "row", None, None))
    return jax.shard_map(body, mesh=mesh, in_specs=in_specs, out_specs=out_specs, check_vma=False)
```

profile of v0, /device:TPU:0, one launch (start us, length us, event | category | flops | bytes accessed | tf_op | source)
XLA Modules:
  0.0 273.2 jit_solution(2087732501633860440)
XLA Ops:
  7.2 1.3 convert_reduce_fusion
  8.9 5.9 %all-reduce.2 = (f32[1,32]{1,0:T(1,128)S(1)}, f32[1,32]{1,0:T(1,128)S(1)}) all-reduce(f32[1,32]{1,0:T(1,128)S(1)} %bitcast.138, f32[1,32]{1,0:T(1,128)S(1)} %bitcast.137), channel_id=1, replica_groups=mesh['asset'=8,'frame'=2,'row'=2] {'row'}, use_global_device_ids=true, to_apply=%region_5.6 | all-reduce | flops 64 | bytes 512 | tf_op jit(solution)/shard_map/psum | solution.py:101
  15.1 1.3 fusion.64
  16.4 4.0 %collective-permute-start = (bf16[1,1,72,1280]{3,2,1,0:T(8,128)(2,1)S(1)}, bf16[1,1,72,1280]{3,2,1,0:T(8,128)(2,1)S(1)}, u32[]{:S(2)}, u32[]{:S(2)}) collective-permute-start(bf16[1,1,72,1280]{3,2,1,0:T(8,128)(2,1)S(1)} %get-tuple-element.23), channel_id=1, source_target_pairs={{0,1},{2,3},{4,5},{6,7},{8,9},{10,11},{12,13},{14,15},{16,17},{18,... | collective-permute-start | bytes 552968 | tf_op jit(solution)/shard_map/ppermute | solution.py:23
  20.4 1.3 collective-permute-start.1
  21.7 1.7 collective-permute-done
  23.4 4.4 %collective-permute-done.1 = bf16[1,1,72,1280]{3,2,1,0:T(8,128)(2,1)S(1)} collective-permute-done((bf16[1,1,72,1280]{3,2,1,0:T(8,128)(2,1)S(1)}, bf16[1,1,72,1280]{3,2,1,0:T(8,128)(2,1)S(1)}, u32[]{:S(2)}, u32[]{:S(2)}) %collective-permute-start.1) | collective-permute-done | bytes 184352 | tf_op jit(solution)/shard_map/ppermute | solution.py:25
  27.8 1.0 pad_maximum_fusion
  30.9 1.2 copy.49
  32.2 3.5 %all-to-all-start = ((bf16[1,2,72,1280]{2,1,0,3:T(2,128)(2,1)}), bf16[1,2,72,1280]{2,1,0,3:T(2,128)(2,1)S(1)}, u32[]{:S(2)}, u32[]{:S(2)}) async-start(bf16[1,2,72,1280]{2,1,0,3:T(2,128)(2,1)} %copy.49), calls=%async_computation | async-start | bytes 1310720 | tf_op jit(solution)/shard_map/all_to_all | solution.py:110
  36.2 8.6 %all-reduce.1 = (f32[32]{0:T(128)S(1)}, f32[32]{0:T(128)S(1)}) all-reduce(f32[32]{0:T(128)S(1)} %reduce_sum.111, f32[32]{0:T(128)S(1)} %reduce_sum.108), channel_id=1, replica_groups=mesh['asset'=8,'frame'=2,'row'=2] {'frame','row'}, use_global_device_ids=true, to_apply=%region_14.15 | all-reduce | flops 64 | bytes 512 | tf_op jit(solution)/shard_map/psum | solution.py:172
  45.9 1.1 collective-permute-start.2
  47.9 2.1 fusion.75
  50.5 5.6 %collective-permute-done.2 = bf16[1,2,72,512]{3,2,1,0:T(8,128)(2,1)S(1)} collective-permute-done((bf16[1,2,72,512]{3,2,1,0:T(8,128)(2,1)}, bf16[1,2,72,512]{3,2,1,0:T(8,128)(2,1)S(1)}, u32[]{:S(2)}, u32[]{:S(2)}) %collective-permute-start.2) | collective-permute-done | bytes 147488 | tf_op jit(solution)/shard_map/ppermute | solution.py:35
  56.2 2.0 fusion.73
  58.6 0.9 copy.50
  59.5 2.6 all-gather.6.cloned.1.call-done
  62.2 4.5 %pad_slice_fusion.1 = (bf16[2,2,72,1280]{3,2,1,0:T(8,128)(2,1)S(1)}, bf16[2,2,72,1280]{3,2,1,0:T(8,128)(2,1)S(1)}, bf16[2,2,72,1280]{3,2,1,0:T(8,128)(2,1)S(1)},...) fusion(bf16[2,4,72,1280]{3,2,1,0:T(8,128)(2,1)} %all-gather.6.c, ...), kind=kLoop, calls=%fused_computation.51 | loop fusion | bytes 10321920 | tf_op jit(solution)/shard_map/slice | solution.py:63
  66.7 2.2 fusion.11
  68.9 2.3 fusion.13
  71.2 2.3 fusion.15
  73.5 2.2 fusion.7
  75.7 2.2 fusion.9
  77.9 2.2 fusion.1
  80.1 2.2 fusion.3
  82.3 2.3 fusion.41
  84.5 2.2 fusion.50
  86.8 1.3 fusion.68
  88.1 3.6 %all-to-all-start.1 = ((bf16[2,144,640]{2,0,1:T(2,128)(2,1)}), bf16[2,144,640]{2,0,1:T(2,128)(2,1)S(1)}, u32[]{:S(2)}, u32[]{:S(2)}) async-start(bf16[2,144,640]{2,0,1:T(2,128)(2,1)} %fusion.68), calls=%async_computation.1 | async-start | bytes 737280 | tf_op jit(solution)/shard_map/all_to_all | solution.py:116
  91.8 2.0 fusion.55
  93.8 9.1 %all-to-all-done.1 = bf16[2,144,640]{2,0,1:T(2,128)(2,1)S(1)} async-done(((bf16[2,144,640]{2,0,1:T(2,128)(2,1)}), bf16[2,144,640]{2,0,1:T(2,128)(2,1)S(1)}, u32[]{:S(2)}, u32[]{:S(2)}) %all-to-all-start.1) | async-done | bytes 368672 | tf_op jit(solution)/shard_map/all_to_all | solution.py:116
  103.4 0.9 bitcast_reduce_fusion
  104.6 7.7 %all-gather.8.cloned.1.call-done = bf16[1280,1280]{1,0:T(8,128)(2,1)} async-done(((bf16[320,1280]{1,0:T(8,128)(2,1)}), bf16[1280,1280]{1,0:T(8,128)(2,1)}) %all-gather.8.cloned.1.call-update) | async-done | bytes 3276816 | tf_op jit(solution)/shard_map/all_gather | solution.py:134
  112.3 2.6 convolution_convert_fusion.2
  115.5 43.6 %all-gather.10.cloned.1.call-done = bf16[1280,1280]{1,0:T(8,128)(2,1)} async-done(((bf16[320,1280]{1,0:T(8,128)(2,1)}), bf16[1280,1280]{1,0:T(8,128)(2,1)}) %all-gather.10.cloned.1.call-update) | async-done | bytes 3276816 | tf_op jit(solution)/shard_map/all_gather | solution.py:132
  159.1 2.6 convolution_convert_fusion.1
  161.8 1.5 reshape.207
  163.3 42.5 %all-gather.12.cloned.1.call-done = bf16[1280,1280]{1,0:T(8,128)(2,1)} async-done(((bf16[320,1280]{1,0:T(8,128)(2,1)}), bf16[1280,1280]{1,0:T(8,128)(2,1)}) %all-gather.12.cloned.1.call-update) | async-done | bytes 3276816 | tf_op jit(solution)/shard_map/all_gather | solution.py:133
  205.8 2.6 convolution_convert_fusion
  208.4 1.5 reshape.208
  210.0 3.1 %fusion.70 = f32[72,20,2,2]{2,3,1,0:T(2,128)S(1)} fusion(bf16[2,72,20,64]{3,2,1,0:T(8,128)(2,1)} %reshape.208, bf16[2,72,20,64]{3,2,1,0:T(8,128)(2,1)} %reshape.207), kind=kOutput, calls=%fused_computation.75 | convolution fusion | flops 737280 | bytes 760320 | tf_op jit(solution)/shard_map/fphd,gphd->phfg/dot_general | solution.py:143
  214.6 1.7 fusion.28
  216.4 1.2 reshape.209
  217.6 34.9 %all-gather.14.cloned.1.call-done = bf16[1280,1280]{1,0:T(8,128)(2,1)} async-done(((bf16[320,1280]{1,0:T(8,128)(2,1)}), bf16[1280,1280]{1,0:T(8,128)(2,1)}) %all-gather.14.cloned.1.call-update) | async-done | bytes 3276816 | tf_op jit(solution)/shard_map/all_gather | solution.py:156
  252.5 3.6 %fusion = bf16[144,1280]{1,0:T(8,128)(2,1)} fusion(f32[144,1280]{1,0:T(8,128)S(1)} %bitcast.117, bf16[144,1280]{1,0:T(8,128)(2,1)} %reshape.209, bf16[1280,1280]{1,0:T(8,128)(2,1)} %all-gather.14.cloned.1.call-done), kind=kOutput, calls=%fused_computation.1 | convolution fusion | flops 472227840 | bytes 4751360 | tf_op jit(solution)/shard_map/dot_general | solution.py:154
  256.0 3.5 %all-to-all-start.2 = ((bf16[2,72,1280]{2,1,0:T(8,128)(2,1)}), bf16[2,72,1280]{2,1,0:T(8,128)(2,1)S(1)}, u32[]{:S(2)}, u32[]{:S(2)}) async-start(bf16[2,72,1280]{2,1,0:T(8,128)(2,1)} %bitcast.126), calls=%async_computation.2 | async-start | bytes 737280 | tf_op jit(solution)/shard_map/all_to_all | solution.py:164
  259.5 1.7 fusion.91
  261.2 4.8 %all-to-all-done.2 = bf16[2,72,1280]{2,1,0:T(8,128)(2,1)S(1)} async-done(((bf16[2,72,1280]{2,1,0:T(8,128)(2,1)}), bf16[2,72,1280]{2,1,0:T(8,128)(2,1)S(1)}, u32[]{:S(2)}, u32[]{:S(2)}) %all-to-all-start.2) | async-done | bytes 368672 | tf_op jit(solution)/shard_map/all_to_all | solution.py:164
  (76 shorter events, 9.4 us)
Async XLA Ops:
  7.2 43.1 %copy-start = (bf16[960,1280]{1,0:T(8,128)(2,1)S(1)}, bf16[960,1280]{1,0:T(8,128)(2,1)}, u32[]{:S(2)}) copy-start(bf16[960,1280]{1,0:T(8,128)(2,1)} %param.22) | copy-start | bytes 7372804
  7.2 55.0 %all-gather.6.cloned.1.call-start = ((), (), s32[]{:S(2)}) async-start(), calls=%async_computation.3 | async-start | bytes 2211840 | tf_op jit(solution)/shard_map/all_gather | solution.py:114
  16.4 7.0 %collective-permute-start = (bf16[1,1,72,1280]{3,2,1,0:T(8,128)(2,1)S(1)}, bf16[1,1,72,1280]{3,2,1,0:T(8,128)(2,1)S(1)}, u32[]{:S(2)}, u32[]{:S(2)}) collective-permute-start(bf16[1,1,72,1280]{3,2,1,0:T(8,128)(2,1)S(1)} %get-tuple-element.23), channel_id=1, source_target_pairs={{0,1},{2,3},{4,5},{6,7},{8,9},{10,11},{12,13},{14,15},{16,17},{18,... | collective-permute-start | bytes 552968 | tf_op jit(solution)/shard_map/ppermute | solution.py:23
  20.4 7.4 %collective-permute-start.1 = (bf16[1,1,72,1280]{3,2,1,0:T(8,128)(2,1)S(1)}, bf16[1,1,72,1280]{3,2,1,0:T(8,128)(2,1)S(1)}, u32[]{:S(2)}, u32[]{:S(2)}) collective-permute-start(bf16[1,1,72,1280]{3,2,1,0:T(8,128)(2,1)S(1)} %get-tuple-element.24), channel_id=1, source_target_pairs={{1,0},{3,2},{5,4},{7,6},{9,8},{11,10},{13,12},{15,14},{17,16},{19,... | collective-permute-start | bytes 552968 | tf_op jit(solution)/shard_map/ppermute | solution.py:25
  28.8 2.1 copy-start.2
  28.8 83.5 %all-gather.8.cloned.1.call-start = ((), (), s32[]{:S(2)}) async-start(), calls=%async_computation.4 | async-start | bytes 4096000 | tf_op jit(solution)/shard_map/all_gather | solution.py:134
  29.5 129.6 %all-gather.10.cloned.1.call-start = ((), (), s32[]{:S(2)}) async-start(), calls=%async_computation.5 | async-start | bytes 4096000 | tf_op jit(solution)/shard_map/all_gather | solution.py:132
  30.3 5.5 %copy-start.3 = (bf16[1,2,72,512]{3,2,1,0:T(8,128)(2,1)S(1)}, bf16[1,2,72,512]{3,2,1,0:T(8,128)(2,1)}, u32[]{:S(2)}) copy-start(bf16[1,2,72,512]{3,2,1,0:T(8,128)(2,1)} %param.19) | copy-start | bytes 442372
  30.3 14.8 %copy-start.8 = (f32[512]{0:T(512)S(1)}, f32[512]{0:T(512)}, u32[]{:S(2)}) copy-start(f32[512]{0:T(512)} %param.30) | copy-start | bytes 6148
  30.3 14.8 %copy-start.9 = (f32[512]{0:T(512)S(1)}, f32[512]{0:T(512)}, u32[]{:S(2)}) copy-start(f32[512]{0:T(512)} %param.29) | copy-start | bytes 6148
  30.3 175.5 %all-gather.12.cloned.1.call-start = ((), (), s32[]{:S(2)}) async-start(), calls=%async_computation.6 | async-start | bytes 4096000 | tf_op jit(solution)/shard_map/all_gather | solution.py:133
  30.9 16.1 %copy-start.7 = (s32[2,2]{1,0:T(2,128)S(1)}, s32[2,2]{1,0:T(2,128)}, u32[]{:S(2)}) copy-start(s32[2,2]{1,0:T(2,128)} %param.18) | copy-start | bytes 52
  32.2 26.0 %all-to-all-start = ((bf16[1,2,72,1280]{2,1,0,3:T(2,128)(2,1)}), bf16[1,2,72,1280]{2,1,0,3:T(2,128)(2,1)S(1)}, u32[]{:S(2)}, u32[]{:S(2)}) async-start(bf16[1,2,72,1280]{2,1,0,3:T(2,128)(2,1)} %copy.49), calls=%async_computation | async-start | bytes 1310720 | tf_op jit(solution)/shard_map/all_to_all | solution.py:110
  35.7 216.8 %all-gather.14.cloned.1.call-start = ((), (), s32[]{:S(2)}) async-start(), calls=%async_computation.7 | async-start | bytes 4096000 | tf_op jit(solution)/shard_map/all_gather | solution.py:156
  45.9 10.3 %collective-permute-start.2 = (bf16[1,2,72,512]{3,2,1,0:T(8,128)(2,1)}, bf16[1,2,72,512]{3,2,1,0:T(8,128)(2,1)S(1)}, u32[]{:S(2)}, u32[]{:S(2)}) collective-permute-start(bf16[1,2,72,512]{3,2,1,0:T(8,128)(2,1)} %fusion.89), channel_id=1, source_target_pairs={{2,0},{0,2},{3,1},{1,3},{6,4},{4,6},{7,5},{5,7},{10,8},{8,10},{11,... | collective-permute-start | bytes 442376 | tf_op jit(solution)/shard_map/ppermute | solution.py:35
  86.7 5.0 %copy-start.4 = (f32[144,512]{1,0:T(8,128)S(1)}, f32[144,512]{1,0:T(8,128)}, u32[]{:S(2)}) copy-start(f32[144,512]{1,0:T(8,128)} %fusion.75) | copy-start | bytes 884740
  86.8 5.0 %copy-start.5 = (f32[144,512]{1,0:T(8,128)S(1)}, f32[144,512]{1,0:T(8,128)}, u32[]{:S(2)}) copy-start(f32[144,512]{1,0:T(8,128)} %fusion.73) | copy-start | bytes 884740
  88.1 14.8 %all-to-all-start.1 = ((bf16[2,144,640]{2,0,1:T(2,128)(2,1)}), bf16[2,144,640]{2,0,1:T(2,128)(2,1)S(1)}, u32[]{:S(2)}, u32[]{:S(2)}) async-start(bf16[2,144,640]{2,0,1:T(2,128)(2,1)} %fusion.68), calls=%async_computation.1 | async-start | bytes 737280 | tf_op jit(solution)/shard_map/all_to_all | solution.py:116
  103.1 9.2 %copy-start.6 = (f32[1280]{0:T(1024)S(1)}, f32[1280]{0:T(1024)}, u32[]{:S(2)}) copy-start(f32[1280]{0:T(1024)} %param.24) | copy-start | bytes 15364
  252.5 14.2 %copy-start.1 = (bf16[960,1280]{1,0:T(8,128)(2,1)S(1)}, bf16[960,1280]{1,0:T(8,128)(2,1)}, u32[]{:S(2)}) copy-start(bf16[960,1280]{1,0:T(8,128)(2,1)} %param.22) | copy-start | bytes 7372804
  256.0 9.9 %all-to-all-start.2 = ((bf16[2,72,1280]{2,1,0:T(8,128)(2,1)}), bf16[2,72,1280]{2,1,0:T(8,128)(2,1)S(1)}, u32[]{:S(2)}, u32[]{:S(2)}) async-start(bf16[2,72,1280]{2,1,0:T(8,128)(2,1)} %bitcast.126), calls=%async_computation.2 | async-start | bytes 737280 | tf_op jit(solution)/shard_map/all_to_all | solution.py:164
Sparse Core Ops, SparseCore 0:
  28.9 33.1 all-gather.5
  64.0 48.2 all-gather.7
  114.2 44.9 all-gather.9
  160.8 44.9 all-gather.11
  207.5 44.9 all-gather.13
where the time goes:
time: 274 us; the launch traced here: 273 us
  waiting for transfers between devices  159 us (58%)
  matrix products  42.6 us (16%)
  starting transfers between devices  17.1 us (6%)
  local copies, waits for them, and re-layouts  15.3 us (6%)
  between operations  14.9 us (5%)
  blocking collectives  14.4 us (5%)
  other arithmetic  9.98 us (4%)
    all_gather x1, waiting for transfers between devices, body(): lax.all_gather(q_weight, ('frame', 'row'), axis=0, tiled=True)  43.6 us
    all_gather x1, waiting for transfers between devices, body(): lax.all_gather(k_weight, ('frame', 'row'), axis=0, tiled=True)  42.5 us
    all_gather x1, waiting for transfers between devices, body(): lax.all_gather(o_weight, ('frame', 'row'), axis=0, tiled=True)  34.9 us
    dot_general x9, matrix products, convolve(): jnp.dot(window, kernel[down, side], preferred_element_type=jnp.float32)  20 us
    all_to_all x1, waiting for transfers between devices, body(): lax.all_to_all(spatial.reshape(frames, band * width, share), 'frame', spl...  9.05 us
    psum x1, blocking collectives, body(): lax.psum((jnp.sum(dec_grouped, axis=(0, 1, 2, 4)), jnp.sum(dec_grouped *...  8.58 us
    dot_general x3, matrix products, body(): jnp.dot(inputs, weight_part, preferred_element_type=jnp.float32)  7.86 us
    all_gather x1, waiting for transfers between devices, body(): lax.all_gather(v_weight, ('frame', 'row'), axis=0, tiled=True)  7.74 us
  transfers between devices with their start and end apart: 11, of which 10 were waited for; matrix products, arithmetic and copies ran while one was open for 22% of the time, Pallas kernels for 0%

commit v1 on v0

--- a/solution.py
+++ b/solution.py
@@ -3,6 +3,8 @@
 import jax
 import jax.numpy as jnp
 from jax import lax
+from jax.experimental import pallas as pl
+from jax.experimental.pallas import tpu as pltpu
 from jax.sharding import PartitionSpec as P
 
 HEADS = 20
@@ -199,6 +201,468 @@
     return (unet_out, dec_out)
 
 
+def silu(x):
+    return x * jax.nn.sigmoid(x)
+
+
+def group_matrix(channels, groups):
+    size = channels // groups
+    channel = lax.broadcasted_iota(jnp.int32, (channels, 128), 0)
+    low = lax.broadcasted_iota(jnp.int32, (channels, 128), 1) * size
+    return jnp.where((channel >= low) & (channel < low + size), 1.0, 0.0).astype(jnp.float32)
+
+
+def group_norm_terms(sums, number, channels):
+    member = group_matrix(channels, G)
+    grouped = jnp.dot(
+        sums, member, precision=lax.Precision.HIGHEST, preferred_element_type=jnp.float32
+    )
+    spread = lax.dot_general(
+        grouped,
+        member,
+        (((1,), (1,)), ((), ())),
+        precision=lax.Precision.HIGHEST,
+        preferred_element_type=jnp.float32,
+    )
+    mean = spread[0:1] / number
+    square = spread[1:2] / number
+    return mean, lax.rsqrt(square - mean * mean + EPSILON)
+
+
+CHUNKS = ((0, 256), (256, 256), (512, 128))
+
+
+def kernel(
+    latent_ref,
+    dec_ref,
+    feats_ref,
+    gain_ref,
+    shift_ref,
+    ln_ref,
+    dgain_ref,
+    dshift_ref,
+    emb_hbm,
+    conv_hbm,
+    wsend_hbm,
+    o_hbm,
+    time_hbm,
+    out_ref,
+    dec_out_ref,
+    convw,
+    emb,
+    ow,
+    timew,
+    latbuf,
+    xcat,
+    spat,
+    wg,
+    decoth,
+    stats,
+    psend,
+    precv,
+    load_sem,
+    lat_send,
+    lat_recv,
+    dec_send,
+    dec_recv,
+    st_send,
+    st_recv,
+    w_send,
+    w_recv,
+    fw_send,
+    fw_recv,
+    sp_send,
+    sp_recv,
+    rs_send,
+    rs_recv,
+):
+    MESH = pl.DeviceIdType.MESH
+    asset = lax.axis_index("asset")
+    f = lax.axis_index("frame")
+    r = lax.axis_index("row")
+    core = asset % 2
+    sibling = asset + 1 - 2 * core
+    me = 2 * f + r
+    _, band, width, channels = latent_ref.shape
+    cells = band * width
+    share = convw.shape[3]
+    rows = ow.shape[0]
+    half = rows // 2
+    dec_channels = dec_ref.shape[3]
+    stride = width + 8
+
+    def peer(k):
+        pf = 1 - f if k >= 2 else f
+        pr = 1 - r if k % 2 else r
+        return pf, pr
+
+    def remote(src, dst, send, recv, k):
+        pf, pr = peer(k)
+        return pltpu.make_async_remote_copy(
+            src_ref=src,
+            dst_ref=dst,
+            send_sem=send,
+            recv_sem=recv,
+            device_id=(asset, pf, pr),
+            device_id_type=MESH,
+        )
+
+    loads = [
+        pltpu.make_async_copy(emb_hbm.at[:, pl.ds(pl.multiple_of(f * share, 128), share)], emb, load_sem.at[0]),
+        pltpu.make_async_copy(conv_hbm.at[0], convw.at[0], load_sem.at[1]),
+        pltpu.make_async_copy(conv_hbm.at[1], convw.at[1], load_sem.at[2]),
+        pltpu.make_async_copy(conv_hbm.at[2], convw.at[2], load_sem.at[3]),
+        pltpu.make_async_copy(time_hbm, timew, load_sem.at[4]),
+        pltpu.make_async_copy(o_hbm, ow, load_sem.at[5]),
+        pltpu.make_async_copy(
+            wsend_hbm.at[me], wg.at[:, pl.ds(pl.multiple_of(me * rows, 16), rows), :], load_sem.at[6]
+        ),
+    ]
+    for load in loads:
+        load.start()
+
+    barrier = pltpu.get_barrier_semaphore()
+    for k in (1, 2, 3):
+        pf, pr = peer(k)
+        pl.semaphore_signal(barrier, inc=1, device_id=(asset, pf, pr), device_id_type=MESH)
+    pl.semaphore_signal(barrier, inc=1, device_id=(sibling, f, r), device_id_type=MESH)
+    pl.semaphore_wait(barrier, 4)
+
+    def latent_copy(k, slot):
+        return remote(latent_ref.at[0], latbuf.at[slot], lat_send.at[k], lat_recv.at[k], k)
+
+    local_latent = pltpu.make_async_copy(latent_ref.at[0], latbuf.at[r], load_sem.at[7])
+
+    @pl.when(f == r)
+    def _():
+        latent_copy(2, r).start()
+        local_latent.start()
+
+    @pl.when(f != r)
+    def _():
+        latent_copy(3, r).start()
+        latent_copy(1, r).start()
+
+    dec_copy = remote(dec_ref.at[0], decoth, dec_send, dec_recv, 2)
+    dec_copy.start()
+
+    dec_own = dec_ref[0].astype(jnp.float32).reshape(cells, dec_channels)
+    dec_sum = jnp.sum(dec_own, axis=0, keepdims=True)
+    dec_square = jnp.sum(dec_own * dec_own, axis=0, keepdims=True)
+    stats[0] = jnp.concatenate(
+        [dec_sum, dec_square, jnp.zeros((6, dec_channels), jnp.float32)], axis=0
+    )
+    stat_copies = [
+        remote(stats.at[0], stats.at[k], st_send.at[k], st_recv.at[k], k) for k in (1, 2, 3)
+    ]
+    for copy in stat_copies:
+        copy.start()
+
+    loads[0].wait()
+    cond = jnp.dot(feats_ref[...], emb[...], preferred_element_type=jnp.float32)[0:1]
+
+    xcat[0:stride, :] = jnp.zeros((stride, 3 * channels), jnp.bfloat16)
+    xcat[5 * stride : 6 * stride, :] = jnp.zeros((stride, 3 * channels), jnp.bfloat16)
+
+    @pl.when(f == r)
+    def _():
+        local_latent.wait()
+        latent_copy(1, 1 - r).wait_recv()
+
+    @pl.when(f != r)
+    def _():
+        latent_copy(2, r).wait_recv()
+        latent_copy(3, 1 - r).wait_recv()
+
+    def weight_copy(k):
+        pf, pr = peer(k)
+        target = 2 * pf + pr
+        mine = pl.ds(pl.multiple_of(core * half, 16), half)
+        there = pl.ds(pl.multiple_of(me * rows + core * half, 16), half)
+        return remote(
+            wsend_hbm.at[target, :, mine, :], wg.at[:, there, :], w_send.at[k], w_recv.at[k], k
+        )
+
+    def weight_forward(k):
+        pf, pr = peer(k)
+        source = 2 * pf + pr
+        piece = pl.ds(pl.multiple_of(source * rows + core * half, 16), half)
+        return pltpu.make_async_remote_copy(
+            src_ref=wg.at[:, piece, :],
+            dst_ref=wg.at[:, piece, :],
+            send_sem=fw_send.at[k],
+            recv_sem=fw_recv.at[k],
+            device_id=(sibling, f, r),
+            device_id_type=MESH,
+        )
+
+    def weight_arrival(k, which):
+        pf, pr = peer(k)
+        source = 2 * pf + pr
+        part = core if which == 0 else 1 - core
+        piece = pl.ds(pl.multiple_of(source * rows + part * half, 16), half)
+        sems = (w_send, w_recv) if which == 0 else (fw_send, fw_recv)
+        return remote(wg.at[:, piece, :], wg.at[:, piece, :], sems[0].at[k], sems[1].at[k], k)
+
+    for k in (3, 1, 2):
+        weight_copy(k).start()
+
+    total = jnp.zeros((1, channels), jnp.float32)
+    square = jnp.zeros((1, channels), jnp.float32)
+    for i in range(2 * band):
+        x = latbuf[i // band, i % band].astype(jnp.float32)
+        total = total + jnp.sum(x, axis=0, keepdims=True)
+        square = square + jnp.sum(x * x, axis=0, keepdims=True)
+    sums = jnp.concatenate([total, square, jnp.zeros((6, channels), jnp.float32)], axis=0)
+    number = float(2 * cells * (channels // G))
+    mean, scale = group_norm_terms(sums, number, channels)
+    for i in range(2 * band):
+        x = latbuf[i // band, i % band].astype(jnp.float32)
+        act = silu((x - mean) * scale * gain_ref[...] + shift_ref[...])
+        padded = jnp.concatenate([act, jnp.zeros((8, channels), jnp.float32)], axis=0)
+        at = slice((i + 1) * stride, (i + 2) * stride)
+        xcat[at, 0:channels] = pltpu.roll(padded, 1, 0).astype(jnp.bfloat16)
+        xcat[at, channels : 2 * channels] = padded.astype(jnp.bfloat16)
+        xcat[at, 2 * channels :] = pltpu.roll(padded, stride - 1, 0).astype(jnp.bfloat16)
+
+    def spatial_copy(k, n, frame, start, size):
+        where = spat.at[frame, :, pl.ds(pl.multiple_of(start, 128), size)]
+        return remote(where, where, sp_send.at[n, k], sp_recv.at[n, k], k)
+
+    for load in loads[1:4]:
+        load.wait()
+    for n, (start, size) in enumerate(CHUNKS):
+
+        def tap(a, acc):
+            lhs = xcat[pl.ds(pl.multiple_of(a * stride, 16), 2 * band * stride), :]
+            rhs = convw[a, :, :, start : start + size].reshape(3 * channels, size)
+            return acc + jnp.dot(lhs, rhs, preferred_element_type=jnp.float32)
+
+        acc = lax.fori_loop(0, 3, tap, jnp.zeros((2 * band * stride, size), jnp.float32))
+        acc = acc.reshape(2 * band, stride, size)[:, :width]
+        column = pl.ds(pl.multiple_of(f * share + start, 128), size)
+        res = latbuf[:, :, :, column].astype(jnp.float32).reshape(2 * band, width, size)
+        new = res + acc + cond[:, start : start + size].reshape(1, 1, size)
+        spat[r, :, column] = new.reshape(2 * cells, size).astype(jnp.bfloat16)
+        for k in (3, 1, 2):
+            spatial_copy(k, n, r, f * share + start, size).start()
+        if n == 1:
+            for k in (3, 1, 2):
+                weight_arrival(k, 0).wait_recv()
+                weight_forward(k).start()
+
+    dec_copy.wait_recv()
+    for copy in stat_copies:
+        copy.wait_recv()
+    dec_total = stats[0] + stats[1] + stats[2] + stats[3]
+    dec_number = float(4 * cells * (dec_channels // G))
+    dmean, dscale = group_norm_terms(dec_total, dec_number, dec_channels)
+
+    def dec_act(x):
+        return silu((x - dmean) * dscale * dgain_ref[...] + dshift_ref[...]).astype(jnp.bfloat16)
+
+    dec_values = dec_ref[0].astype(jnp.float32).reshape(cells, dec_channels)
+    middle = dec_act(dec_values)
+    around = dec_act(decoth[...].astype(jnp.float32).reshape(cells, dec_channels))
+    loads[4].wait()
+    temporal = jnp.dot(around, timew[0], preferred_element_type=jnp.float32)
+    temporal = temporal + jnp.dot(middle, timew[1], preferred_element_type=jnp.float32)
+    temporal = temporal + jnp.dot(around, timew[2], preferred_element_type=jnp.float32)
+    dec_out_ref[0] = (
+        (dec_values + temporal).reshape(band, width, dec_channels).astype(jnp.bfloat16)
+    )
+
+    head_size = channels // HEADS
+    lane = lax.broadcasted_iota(jnp.int32, (rows, 128), 0)
+    low = lax.broadcasted_iota(jnp.int32, (rows, 128), 1) * head_size
+    member = jnp.where((lane >= low) & (lane < low + head_size), 1.0, 0.0).astype(jnp.bfloat16)
+    loads[5].wait()
+    loads[6].wait()
+    for n, (start, size) in enumerate(CHUNKS):
+        for k in (1, 2, 3):
+            pf, pr = peer(k)
+            spatial_copy(k, n, pr, pf * share + start, size).wait_recv()
+    for k in (3, 1, 2):
+        weight_arrival(k, 1).wait_recv()
+
+    def share_of(which):
+        where = pl.ds(pl.multiple_of(which * cells, 16), cells)
+        tokens = jnp.concatenate([spat[0, where, :], spat[1, where, :]], axis=0).astype(jnp.float32)
+        mean = jnp.mean(tokens, axis=-1, keepdims=True)
+        square = jnp.mean(tokens * tokens, axis=-1, keepdims=True)
+        scale = lax.rsqrt(square - mean * mean + EPSILON)
+        normal = ((tokens - mean) * scale * ln_ref[...]).astype(jnp.bfloat16)
+        q, k, v = [
+            jnp.dot(normal, wg[i], preferred_element_type=jnp.float32)
+            .astype(jnp.bfloat16)
+            .astype(jnp.float32)
+            for i in range(3)
+        ]
+        high, rest = [], []
+        for a in range(2):
+            for b in range(2):
+                product = q[a * cells : (a + 1) * cells] * k[b * cells : (b + 1) * cells]
+                top = product.astype(jnp.bfloat16)
+                high.append(top)
+                rest.append((product - top.astype(jnp.float32)).astype(jnp.bfloat16))
+        dots = jnp.dot(
+            jnp.concatenate(high + rest, axis=0), member, preferred_element_type=jnp.float32
+        )
+        scores = (dots[: 4 * cells] + dots[4 * cells :]) * (1.0 / math.sqrt(head_size))
+        weights = jnp.exp(scores)
+        probs = []
+        for a in range(2):
+            pair = [weights[(2 * a + b) * cells : (2 * a + b + 1) * cells] for b in range(2)]
+            bottom = pair[0] + pair[1]
+            probs += [(one / bottom).astype(jnp.bfloat16) for one in pair]
+        spread = lax.dot_general(
+            jnp.concatenate(probs, axis=0),
+            member,
+            (((1,), (1,)), ((), ())),
+            preferred_element_type=jnp.float32,
+        )
+        mixed = [
+            spread[2 * a * cells : (2 * a + 1) * cells] * v[:cells]
+            + spread[(2 * a + 1) * cells : (2 * a + 2) * cells] * v[cells:]
+            for a in range(2)
+        ]
+        mixed = jnp.concatenate(mixed, axis=0).astype(jnp.bfloat16)
+        return jnp.dot(mixed, ow[...], preferred_element_type=jnp.float32)
+
+    def result_copy(k):
+        return remote(psend.at[k], precv.at[k], rs_send.at[k], rs_recv.at[k], k)
+
+    def tokens_of(frame):
+        return pl.ds(pl.multiple_of(frame * cells, 8), cells)
+
+    other = share_of(1 - r).astype(jnp.bfloat16)
+    far = jnp.where(f == 0, other[cells:], other[:cells])
+    near = jnp.where(f == 0, other[:cells], other[cells:])
+    psend[3] = far
+    result_copy(3).start()
+    psend[1] = near
+    result_copy(1).start()
+    own = share_of(r)
+    psend[2] = jnp.where(f == 0, own[cells:], own[:cells]).astype(jnp.bfloat16)
+    result_copy(2).start()
+    mine = jnp.where(f == 0, own[:cells], own[cells:])
+    where = pl.ds(pl.multiple_of(r * cells, 16), cells)
+    result = spat[f, where, :].astype(jnp.float32) + mine
+    for k in (3, 1, 2):
+        result_copy(k).wait_recv()
+        result = result + precv[k].astype(jnp.float32)
+    out_ref[0] = result.reshape(band, width, channels).astype(jnp.bfloat16)
+
+    @pl.when(f == r)
+    def _():
+        latent_copy(2, r).wait_send()
+
+    @pl.when(f != r)
+    def _():
+        latent_copy(3, r).wait_send()
+        latent_copy(1, r).wait_send()
+
+    dec_copy.wait_send()
+    for copy in stat_copies:
+        copy.wait_send()
+    for k in (1, 2, 3):
+        weight_copy(k).wait_send()
+        weight_forward(k).wait_send()
+        result_copy(k).wait_send()
+        for n, (start, size) in enumerate(CHUNKS):
+            spatial_copy(k, n, r, f * share + start, size).wait_send()
+
+
+def fused(
+    latent,
+    timestep,
+    camera,
+    dec_feat,
+    norm_gain,
+    norm_shift,
+    emb_weight,
+    conv_weight,
+    ln_gain,
+    q_weight,
+    k_weight,
+    v_weight,
+    o_weight,
+    dec_gain,
+    dec_shift,
+    time_weight,
+):
+    _, band, width, channels = latent.shape
+    share = conv_weight.shape[3]
+    rows = q_weight.shape[0]
+    cells = band * width
+    dec_channels = dec_feat.shape[3]
+    features = conditions(timestep, camera, 2, emb_weight.shape[0] // 3)
+    feats = lax.dynamic_slice_in_dim(features, lax.axis_index("row"), 1, 0)
+    feats = jnp.broadcast_to(feats, (16, feats.shape[1]))
+    wsend = jnp.stack([q_weight, k_weight, v_weight]).reshape(3, rows, 4, rows)
+    wsend = wsend.transpose(2, 0, 1, 3)
+    vmem = pl.BlockSpec(memory_space=pltpu.VMEM)
+    hbm = pl.BlockSpec(memory_space=pl.ANY)
+    dma = pltpu.SemaphoreType.DMA
+    bf16, f32 = jnp.bfloat16, jnp.float32
+    return pl.pallas_call(
+        kernel,
+        out_shape=(
+            jax.ShapeDtypeStruct(latent.shape, bf16),
+            jax.ShapeDtypeStruct(dec_feat.shape, bf16),
+        ),
+        in_specs=[vmem] * 8 + [hbm] * 5,
+        out_specs=(vmem, vmem),
+        scratch_shapes=[
+            pltpu.VMEM(conv_weight.shape, bf16),
+            pltpu.VMEM((emb_weight.shape[0], share), bf16),
+            pltpu.VMEM(o_weight.shape, bf16),
+            pltpu.VMEM(time_weight.shape, bf16),
+            pltpu.VMEM((2, band, width, channels), bf16),
+            pltpu.VMEM((6 * (width + 8), 3 * channels), bf16),
+            pltpu.VMEM((2, 2 * cells, channels), bf16),
+            pltpu.VMEM((3, channels, rows), bf16),
+            pltpu.VMEM((band, width, dec_channels), bf16),
+            pltpu.VMEM((4, 8, dec_channels), f32),
+            pltpu.VMEM((4, cells, channels), bf16),
+            pltpu.VMEM((4, cells, channels), bf16),
+            dma((8,)),
+            dma((4,)),
+            dma((4,)),
+            dma,
+            dma,
+            dma((4,)),
+            dma((4,)),
+            dma((4,)),
+            dma((4,)),
+            dma((4,)),
+            dma((4,)),
+            dma((3, 4)),
+            dma((3, 4)),
+            dma((4,)),
+            dma((4,)),
+        ],
+        compiler_params=pltpu.CompilerParams(
+            collective_id=0, has_side_effects=True, vmem_limit_bytes=60 * 1024 * 1024
+        ),
+        name="denoise",
+    )(
+        latent,
+        dec_feat,
+        feats,
+        norm_gain.reshape(1, -1),
+        norm_shift.reshape(1, -1),
+        ln_gain.reshape(1, -1),
+        dec_gain.reshape(1, -1),
+        dec_shift.reshape(1, -1),
+        emb_weight,
+        conv_weight,
+        wsend,
+        o_weight,
+        time_weight,
+    )
+
+
 def solution(mesh):
     in_specs = (
         P(("asset", "frame"), "row", None, None),
@@ -219,4 +683,6 @@
         P(),
     )
     out_specs = (P(("asset", "frame"), "row", None, None), P(("asset", "frame"), "row", None, None))
-    return jax.shard_map(body, mesh=mesh, in_specs=in_specs, out_specs=out_specs, check_vma=False)
+    sizes = dict(mesh.shape)
+    small = sizes["frame"] == 2 and sizes["row"] == 2 and sizes["asset"] % 2 == 0
+    return jax.shard_map(fused if small else body, mesh=mesh, in_specs=in_specs, out_specs=out_specs, check_vma=False)

time: 274 us -> 96.1 us (0.35)
  waiting for transfers between devices: 159 us -> 0 us
  Pallas kernels: 0 us -> 78.6 us
  matrix products: 42.6 us -> 0 us
  starting transfers between devices: 17.1 us -> 0 us
  blocking collectives: 14.4 us -> 0 us
  between operations: 14.9 us -> 1.42 us
  other arithmetic: 9.98 us -> 3.45 us
  local copies, waits for them, and re-layouts: 15.3 us -> 12.4 us
    all_gather x5 -> x0, waiting for transfers between devices: 131 us -> none  [the longest x1 43.6 us: body(): lax.all_gather(q_weight, ('frame', 'row'), axis=0, tiled=True)]
    pallas_call x0 -> x1, Pallas kernels: none -> 78.6 us  [fused(): pl.pallas_call(kernel, out_shape=(jax.ShapeDtypeStruct(latent.shape, bf16...]
    dot_general x19 -> x0, matrix products: 42.6 us -> none  [the longest x9 20 us: convolve(): jnp.dot(window, kernel[down, side], preferred_element_type=jnp.float32)]
    psum x2 -> x0, blocking collectives: 14.4 us -> none  [the longest x1 8.58 us: body(): lax.psum((jnp.sum(dec_grouped, axis=(0, 1, 2, 4)), jnp.sum(dec_grouped *...]
    all_to_all x3 -> x0, waiting for transfers between devices: 13.8 us -> none  [the longest x1 9.05 us: body(): lax.all_to_all(spatial.reshape(frames, band * width, share), 'frame', spl...]
    ppermute x3 -> x0, waiting for transfers between devices: 11.8 us -> none  [the longest x1 5.64 us: from_behind(): return lax.ppermute(block, axis, route)]
    all_to_all x3 -> x0, starting transfers between devices: 10.6 us -> none  [the longest x1 3.64 us: body(): lax.all_to_all(spatial.reshape(frames, band * width, share), 'frame', spl...]
    another operation x0 -> x6, local copies, waits for them, and re-layouts: none -> 6.51 us  [fused(): wsend = jnp.stack([q_weight, k_weight, v_weight]).reshape(3, rows, 4, rows)]
  transfers between devices with their start and end apart: 11 -> 0, of which waited for: 10 -> 0; matrix products, arithmetic and copies ran while one was open for 22% -> 0% of each run, Pallas kernels for 0% -> 0%
where the time goes in v1:
time: 96.1 us; the launch traced here: 95.8 us
  Pallas kernels  78.6 us (82%)
  local copies, waits for them, and re-layouts  12.4 us (13%)
  other arithmetic  3.45 us (4%)
  between operations  1.42 us (1%)
    pallas_call x1, Pallas kernels, fused(): pl.pallas_call(kernel, out_shape=(jax.ShapeDtypeStruct(latent.shape, bf16...  78.6 us
    another operation x6, local copies, waits for them, and re-layouts, fused(): wsend = jnp.stack([q_weight, k_weight, v_weight]).reshape(3, rows, 4, rows)  6.51 us
    unnamed x10, local copies, waits for them, and re-layouts  3.35 us
    transpose x1, other arithmetic, fused(): wsend = wsend.transpose(2, 0, 1, 3)  2.22 us

profile of v1, /device:TPU:0, one launch (start us, length us, event | category | flops | bytes accessed | tf_op | source)
XLA Modules:
  0.0 95.8 jit_solution(885697535031325442)
XLA Ops:
  0.6 0.0 copy-start
  0.6 1.0 %convert_reduce_fusion.1 = (f32[2]{0:T(128)S(1)}, f32[2]{0:T(128)S(1)}) fusion(s32[2,2]{1,0:T(2,128)} %param.18), kind=kLoop, calls=%fused_computation.7 | loop fusion | flops 4 | bytes 32 | tf_op jit(solution)/shard_map/convert_element_type | solution.py:43
  1.6 0.1 multiply_sine_fusion
  2.5 0.1 concatenate.4
  2.7 0.6 broadcast_in_dim.5.feats_ref
  3.3 2.5 %stack.12 = bf16[1,320,4,320]{3,2,1,0:T(4,128)(2,1)S(1)} reshape(bf16[320,1280]{1,0:T(8,128)(2,1)} %param.25) | data formatting | bytes 1638400 | tf_op jit(solution)/shard_map/stack | solution.py:602
  5.8 0.1 copy.18
  6.0 0.0 copy-done
  6.0 1.1 %stack.13 = bf16[1,320,4,320]{3,2,1,0:T(4,128)(2,1)S(1)} reshape(bf16[320,1280]{1,0:T(8,128)(2,1)S(1)} %copy-done) | data formatting | bytes 1638400 | tf_op jit(solution)/shard_map/stack | solution.py:602
  7.0 0.1 copy.19
  7.2 2.5 %stack.14 = bf16[1,320,4,320]{3,2,1,0:T(4,128)(2,1)S(1)} reshape(bf16[320,1280]{1,0:T(8,128)(2,1)} %param.27) | data formatting | bytes 1638400 | tf_op jit(solution)/shard_map/stack | solution.py:602
  9.7 0.1 copy.20
  9.9 0.0 copy-start.1
  9.9 0.0 copy-start.2
  9.9 0.0 copy-start.3
  9.9 2.2 %maximum_bitcast_fusion.wsend_hbm = bf16[4,3,320,320]{3,2,1,0:T(8,128)(2,1)} fusion(bf16[1,320,4,320]{3,1,0,2:T(8,128)(2,1)S(1)} %copy.20, bf16[1,320,4,320]{3,1,0,2:T(8,128)(2,1)S(1)} %copy.19, bf16[1,320,4,320]{3,1,0,2:T(8,128)(2,1)S(1)} %copy.18), kind=kLoop, calls=%fused_computation | loop fusion | flops 2457600 | bytes 4915200 | tf_op jit(solution)/shard_map/transpose | solution.py:603
  12.1 0.0 copy-done.1
  12.1 0.6 reshape.32.gain_ref
  12.7 0.0 copy-done.2
  12.7 0.6 reshape.33.shift_ref
  13.3 0.0 copy-done.3
  13.3 0.6 reshape.34.ln_ref
  13.9 78.6 %denoise.1 = (bf16[1,2,72,1280]{3,2,1,0:T(8,128)(2,1)}, bf16[1,2,72,512]{3,2,1,0:T(8,128)(2,1)}) custom-call(bf16[1,2,72,1280]{3,2,1,0:T(8,128)(2,1)} %latent_ref.1, bf16[1,2,72,512]{3,2,1,0:T(8,128)(2,1)} %dec_ref.1, bf16[16,960]{1,0:T(8,128)(2,1)} %broadcast_in_dim.5.feats_ref, f32[1,1280]{1,0:T(1,128)} %reshape.32.gain_ref, f32[1,1280]{1,0:T(1,128)} %reshape.33.shift_ref, ...), custom_call_target="tpu_custom_call" | custom-call | tf_op jit(solution)/shard_map/denoise/pallas_call | solution.py:608
  92.5 1.7 %copy.24 = bf16[1,2,72,1280]{3,2,1,0:T(8,128)(2,1)} copy(bf16[1,2,72,1280]{3,2,1,0:T(8,128)(2,1)} %get-tuple-element.14) | data formatting | bytes 737280
  94.2 1.6 %copy.25 = bf16[1,2,72,512]{3,2,1,0:T(8,128)(2,1)} copy(bf16[1,2,72,512]{3,2,1,0:T(8,128)(2,1)} %get-tuple-element.15) | data formatting | bytes 294912
  (5 shorter events, 0.1 us)
Async XLA Ops:
  0.6 5.3 %copy-start = (bf16[320,1280]{1,0:T(8,128)(2,1)S(1)}, bf16[320,1280]{1,0:T(8,128)(2,1)}, u32[]{:S(2)}) copy-start(bf16[320,1280]{1,0:T(8,128)(2,1)} %param.26) | copy-start | bytes 2457604
  9.9 2.3 %copy-start.1 = (f32[1280]{0:T(1024)S(1)}, f32[1280]{0:T(1024)}, u32[]{:S(2)}) copy-start(f32[1280]{0:T(1024)} %param.20) | copy-start | bytes 15364
  9.9 2.8 %copy-start.2 = (f32[1280]{0:T(1024)S(1)}, f32[1280]{0:T(1024)}, u32[]{:S(2)}) copy-start(f32[1280]{0:T(1024)} %param.21) | copy-start | bytes 15364
  9.9 3.4 %copy-start.3 = (f32[1280]{0:T(1024)S(1)}, f32[1280]{0:T(1024)}, u32[]{:S(2)}) copy-start(f32[1280]{0:T(1024)} %param.24) | copy-start | bytes 15364

commit v2 on v1

--- a/solution.py
+++ b/solution.py
@@ -243,11 +243,16 @@
     dshift_ref,
     emb_hbm,
     conv_hbm,
-    wsend_hbm,
+    q_hbm,
+    k_hbm,
+    v_hbm,
     o_hbm,
     time_hbm,
     out_ref,
     dec_out_ref,
+    wraw,
+    wsend,
+    relay,
     convw,
     emb,
     ow,
@@ -269,8 +274,12 @@
     st_recv,
     w_send,
     w_recv,
+    zw_send,
+    zw_recv,
     fw_send,
     fw_recv,
+    rl_send,
+    rl_recv,
     sp_send,
     sp_recv,
     rs_send,
@@ -281,13 +290,17 @@
     f = lax.axis_index("frame")
     r = lax.axis_index("row")
     core = asset % 2
+    plane = asset // 2 % 2
     sibling = asset + 1 - 2 * core
+    above = asset + 2 - 4 * plane
     me = 2 * f + r
     _, band, width, channels = latent_ref.shape
     cells = band * width
     share = convw.shape[3]
     rows = ow.shape[0]
-    half = rows // 2
+    quarter = rows // 4
+    part = 2 * plane + core
+    part_above = 2 * (1 - plane) + core
     dec_channels = dec_ref.shape[3]
     stride = width + 8
 
@@ -307,16 +320,21 @@
             device_id_type=MESH,
         )
 
+    raw = [
+        pltpu.make_async_copy(ref, wraw.at[i], load_sem.at[8 + i])
+        for i, ref in enumerate((q_hbm, k_hbm, v_hbm))
+    ]
+    for load in raw:
+        load.start()
     loads = [
-        pltpu.make_async_copy(emb_hbm.at[:, pl.ds(pl.multiple_of(f * share, 128), share)], emb, load_sem.at[0]),
+        pltpu.make_async_copy(
+            emb_hbm.at[:, pl.ds(pl.multiple_of(f * share, 128), share)], emb, load_sem.at[0]
+        ),
         pltpu.make_async_copy(conv_hbm.at[0], convw.at[0], load_sem.at[1]),
         pltpu.make_async_copy(conv_hbm.at[1], convw.at[1], load_sem.at[2]),
         pltpu.make_async_copy(conv_hbm.at[2], convw.at[2], load_sem.at[3]),
         pltpu.make_async_copy(time_hbm, timew, load_sem.at[4]),
         pltpu.make_async_copy(o_hbm, ow, load_sem.at[5]),
-        pltpu.make_async_copy(
-            wsend_hbm.at[me], wg.at[:, pl.ds(pl.multiple_of(me * rows, 16), rows), :], load_sem.at[6]
-        ),
     ]
     for load in loads:
         load.start()
@@ -325,13 +343,20 @@
     for k in (1, 2, 3):
         pf, pr = peer(k)
         pl.semaphore_signal(barrier, inc=1, device_id=(asset, pf, pr), device_id_type=MESH)
-    pl.semaphore_signal(barrier, inc=1, device_id=(sibling, f, r), device_id_type=MESH)
-    pl.semaphore_wait(barrier, 4)
+    for other_asset in (sibling, above):
+        pl.semaphore_signal(barrier, inc=1, device_id=(other_asset, f, r), device_id_type=MESH)
+    pl.semaphore_wait(barrier, 5)
 
     def latent_copy(k, slot):
         return remote(latent_ref.at[0], latbuf.at[slot], lat_send.at[k], lat_recv.at[k], k)
 
     local_latent = pltpu.make_async_copy(latent_ref.at[0], latbuf.at[r], load_sem.at[7])
+
+    def relay_copy(i):
+        return remote(latent_ref.at[0, i], relay.at[i], rl_send.at[i], rl_recv.at[i], 2)
+
+    def relay_forward(i, slot):
+        return remote(relay.at[i], latbuf.at[slot, i], rl_send.at[i], rl_recv.at[i], 1)
 
     @pl.when(f == r)
     def _():
@@ -340,7 +365,8 @@
 
     @pl.when(f != r)
     def _():
-        latent_copy(3, r).start()
+        for i in range(band):
+            relay_copy(i).start()
         latent_copy(1, r).start()
 
     dec_copy = remote(dec_ref.at[0], decoth, dec_send, dec_recv, 2)
@@ -358,6 +384,16 @@
     for copy in stat_copies:
         copy.start()
 
+    for load in raw:
+        load.wait()
+    for i in range(3):
+        for target in range(4):
+            wsend[target, i] = wraw[i, :, target * rows : (target + 1) * rows]
+    local_weight = pltpu.make_async_copy(
+        wsend.at[me], wg.at[:, pl.ds(pl.multiple_of(me * rows, 16), rows), :], load_sem.at[6]
+    )
+    local_weight.start()
+
     loads[0].wait()
     cond = jnp.dot(feats_ref[...], emb[...], preferred_element_type=jnp.float32)[0:1]
 
@@ -367,42 +403,51 @@
     @pl.when(f == r)
     def _():
         local_latent.wait()
+        for i in range(band):
+            relay_copy(i).wait_recv()
+            relay_forward(i, r).start()
         latent_copy(1, 1 - r).wait_recv()
 
     @pl.when(f != r)
     def _():
         latent_copy(2, r).wait_recv()
-        latent_copy(3, 1 - r).wait_recv()
+        for i in range(band):
+            relay_forward(i, 1 - r).wait_recv()
+
+    def source_rows(k, which):
+        pf, pr = peer(k)
+        source = 2 * pf + pr
+        return pl.ds(pl.multiple_of(source * rows + which * quarter, 16), quarter)
 
     def weight_copy(k):
         pf, pr = peer(k)
         target = 2 * pf + pr
-        mine = pl.ds(pl.multiple_of(core * half, 16), half)
-        there = pl.ds(pl.multiple_of(me * rows + core * half, 16), half)
+        mine = pl.ds(pl.multiple_of(part * quarter, 16), quarter)
+        there = pl.ds(pl.multiple_of(me * rows + part * quarter, 16), quarter)
         return remote(
-            wsend_hbm.at[target, :, mine, :], wg.at[:, there, :], w_send.at[k], w_recv.at[k], k
+            wsend.at[target, :, mine, :], wg.at[:, there, :], w_send.at[k], w_recv.at[k], k
         )
 
-    def weight_forward(k):
-        pf, pr = peer(k)
-        source = 2 * pf + pr
-        piece = pl.ds(pl.multiple_of(source * rows + core * half, 16), half)
+    def weight_arrival(k):
+        where = wg.at[:, source_rows(k, part), :]
+        return remote(where, where, w_send.at[k], w_recv.at[k], k)
+
+    def weight_pass(k, which, send, recv, other_asset):
+        where = wg.at[:, source_rows(k, which), :]
         return pltpu.make_async_remote_copy(
-            src_ref=wg.at[:, piece, :],
-            dst_ref=wg.at[:, piece, :],
-            send_sem=fw_send.at[k],
-            recv_sem=fw_recv.at[k],
-            device_id=(sibling, f, r),
+            src_ref=where,
+            dst_ref=where,
+            send_sem=send,
+            recv_sem=recv,
+            device_id=(other_asset, f, r),
             device_id_type=MESH,
         )
 
-    def weight_arrival(k, which):
-        pf, pr = peer(k)
-        source = 2 * pf + pr
-        part = core if which == 0 else 1 - core
-        piece = pl.ds(pl.multiple_of(source * rows + part * half, 16), half)
-        sems = (w_send, w_recv) if which == 0 else (fw_send, fw_recv)
-        return remote(wg.at[:, piece, :], wg.at[:, piece, :], sems[0].at[k], sems[1].at[k], k)
+    def weight_up(k, which):
+        return weight_pass(k, which, zw_send.at[k], zw_recv.at[k], above)
+
+    def weight_side(k, j, which):
+        return weight_pass(k, which, fw_send.at[j, k], fw_recv.at[j, k], sibling)
 
     for k in (3, 1, 2):
         weight_copy(k).start()
@@ -418,7 +463,7 @@
     mean, scale = group_norm_terms(sums, number, channels)
     for i in range(2 * band):
         x = latbuf[i // band, i % band].astype(jnp.float32)
-        act = silu((x - mean) * scale * gain_ref[...] + shift_ref[...])
+        act = silu((x - mean) * scale * gain_ref[...].reshape(1, -1) + shift_ref[...].reshape(1, -1))
         padded = jnp.concatenate([act, jnp.zeros((8, channels), jnp.float32)], axis=0)
         at = slice((i + 1) * stride, (i + 2) * stride)
         xcat[at, 0:channels] = pltpu.roll(padded, 1, 0).astype(jnp.bfloat16)
@@ -448,8 +493,9 @@
             spatial_copy(k, n, r, f * share + start, size).start()
         if n == 1:
             for k in (3, 1, 2):
-                weight_arrival(k, 0).wait_recv()
-                weight_forward(k).start()
+                weight_arrival(k).wait_recv()
+                weight_up(k, part).start()
+                weight_side(k, 0, part).start()
 
     dec_copy.wait_recv()
     for copy in stat_copies:
@@ -459,7 +505,7 @@
     dmean, dscale = group_norm_terms(dec_total, dec_number, dec_channels)
 
     def dec_act(x):
-        return silu((x - dmean) * dscale * dgain_ref[...] + dshift_ref[...]).astype(jnp.bfloat16)
+        return silu((x - dmean) * dscale * dgain_ref[...].reshape(1, -1) + dshift_ref[...].reshape(1, -1)).astype(jnp.bfloat16)
 
     dec_values = dec_ref[0].astype(jnp.float32).reshape(cells, dec_channels)
     middle = dec_act(dec_values)
@@ -477,13 +523,17 @@
     low = lax.broadcasted_iota(jnp.int32, (rows, 128), 1) * head_size
     member = jnp.where((lane >= low) & (lane < low + head_size), 1.0, 0.0).astype(jnp.bfloat16)
     loads[5].wait()
-    loads[6].wait()
+    local_weight.wait()
+    for k in (3, 1, 2):
+        weight_up(k, part_above).wait_recv()
+        weight_side(k, 1, part_above).start()
     for n, (start, size) in enumerate(CHUNKS):
         for k in (1, 2, 3):
             pf, pr = peer(k)
             spatial_copy(k, n, pr, pf * share + start, size).wait_recv()
     for k in (3, 1, 2):
-        weight_arrival(k, 1).wait_recv()
+        weight_side(k, 0, 2 * plane + 1 - core).wait_recv()
+        weight_side(k, 1, 2 * (1 - plane) + 1 - core).wait_recv()
 
     def share_of(which):
         where = pl.ds(pl.multiple_of(which * cells, 16), cells)
@@ -491,7 +541,7 @@
         mean = jnp.mean(tokens, axis=-1, keepdims=True)
         square = jnp.mean(tokens * tokens, axis=-1, keepdims=True)
         scale = lax.rsqrt(square - mean * mean + EPSILON)
-        normal = ((tokens - mean) * scale * ln_ref[...]).astype(jnp.bfloat16)
+        normal = ((tokens - mean) * scale * ln_ref[...].reshape(1, -1)).astype(jnp.bfloat16)
         q, k, v = [
             jnp.dot(normal, wg[i], preferred_element_type=jnp.float32)
             .astype(jnp.bfloat16)
@@ -556,10 +606,13 @@
     @pl.when(f == r)
     def _():
         latent_copy(2, r).wait_send()
+        for i in range(band):
+            relay_forward(i, r).wait_send()
 
     @pl.when(f != r)
     def _():
-        latent_copy(3, r).wait_send()
+        for i in range(band):
+            relay_copy(i).wait_send()
         latent_copy(1, r).wait_send()
 
     dec_copy.wait_send()
@@ -567,10 +620,23 @@
         copy.wait_send()
     for k in (1, 2, 3):
         weight_copy(k).wait_send()
-        weight_forward(k).wait_send()
+        weight_up(k, part).wait_send()
+        weight_side(k, 0, part).wait_send()
+        weight_side(k, 1, part_above).wait_send()
         result_copy(k).wait_send()
         for n, (start, size) in enumerate(CHUNKS):
             spatial_copy(k, n, r, f * share + start, size).wait_send()
+
+
+def place(unet_ref, dec_ref, unet_out, dec_out, sem):
+    copies = [
+        pltpu.make_async_copy(unet_ref, unet_out, sem.at[0]),
+        pltpu.make_async_copy(dec_ref, dec_out, sem.at[1]),
+    ]
+    for copy in copies:
+        copy.start()
+    for copy in copies:
+        copy.wait()
 
 
 def fused(
@@ -599,21 +665,22 @@
     features = conditions(timestep, camera, 2, emb_weight.shape[0] // 3)
     feats = lax.dynamic_slice_in_dim(features, lax.axis_index("row"), 1, 0)
     feats = jnp.broadcast_to(feats, (16, feats.shape[1]))
-    wsend = jnp.stack([q_weight, k_weight, v_weight]).reshape(3, rows, 4, rows)
-    wsend = wsend.transpose(2, 0, 1, 3)
     vmem = pl.BlockSpec(memory_space=pltpu.VMEM)
     hbm = pl.BlockSpec(memory_space=pl.ANY)
     dma = pltpu.SemaphoreType.DMA
     bf16, f32 = jnp.bfloat16, jnp.float32
-    return pl.pallas_call(
+    unet, dec = pl.pallas_call(
         kernel,
         out_shape=(
             jax.ShapeDtypeStruct(latent.shape, bf16),
             jax.ShapeDtypeStruct(dec_feat.shape, bf16),
         ),
-        in_specs=[vmem] * 8 + [hbm] * 5,
+        in_specs=[vmem] * 8 + [hbm] * 7,
         out_specs=(vmem, vmem),
         scratch_shapes=[
+            pltpu.VMEM((3, rows, channels), bf16),
+            pltpu.VMEM((4, 3, rows, rows), bf16),
+            pltpu.VMEM((band, width, channels), bf16),
             pltpu.VMEM(conv_weight.shape, bf16),
             pltpu.VMEM((emb_weight.shape[0], share), bf16),
             pltpu.VMEM(o_weight.shape, bf16),
@@ -626,7 +693,7 @@
             pltpu.VMEM((4, 8, dec_channels), f32),
             pltpu.VMEM((4, cells, channels), bf16),
             pltpu.VMEM((4, cells, channels), bf16),
-            dma((8,)),
+            dma((11,)),
             dma((4,)),
             dma((4,)),
             dma,
@@ -637,6 +704,10 @@
             dma((4,)),
             dma((4,)),
             dma((4,)),
+            dma((2, 4)),
+            dma((2, 4)),
+            dma((band,)),
+            dma((band,)),
             dma((3, 4)),
             dma((3, 4)),
             dma((4,)),
@@ -650,17 +721,30 @@
         latent,
         dec_feat,
         feats,
-        norm_gain.reshape(1, -1),
-        norm_shift.reshape(1, -1),
-        ln_gain.reshape(1, -1),
-        dec_gain.reshape(1, -1),
-        dec_shift.reshape(1, -1),
+        norm_gain,
+        norm_shift,
+        ln_gain,
+        dec_gain,
+        dec_shift,
         emb_weight,
         conv_weight,
-        wsend,
+        q_weight,
+        k_weight,
+        v_weight,
         o_weight,
         time_weight,
     )
+    return pl.pallas_call(
+        place,
+        out_shape=(
+            jax.ShapeDtypeStruct(latent.shape, bf16),
+            jax.ShapeDtypeStruct(dec_feat.shape, bf16),
+        ),
+        in_specs=[vmem, vmem],
+        out_specs=(hbm, hbm),
+        scratch_shapes=[dma((2,))],
+        name="place",
+    )(unet, dec)
 
 
 def solution(mesh):
@@ -684,5 +768,5 @@
     )
     out_specs = (P(("asset", "frame"), "row", None, None), P(("asset", "frame"), "row", None, None))
     sizes = dict(mesh.shape)
-    small = sizes["frame"] == 2 and sizes["row"] == 2 and sizes["asset"] % 2 == 0
+    small = sizes["frame"] == 2 and sizes["row"] == 2 and sizes["asset"] % 4 == 0
     return jax.shard_map(fused if small else body, mesh=mesh, in_specs=in_specs, out_specs=out_specs, check_vma=False)

time: 96.1 us -> 69.2 us (0.72)
  Pallas kernels: 78.6 us -> 65.8 us
  local copies, waits for them, and re-layouts: 12.4 us -> 0.73 us
  other arithmetic: 3.45 us -> 1.22 us
    pallas_call x1, Pallas kernels: 78.6 us -> 64 us  [fused(): pl.pallas_call(kernel, out_shape=(jax.ShapeDtypeStruct(latent.shape, bf16...]
    another operation x6 -> x0, local copies, waits for them, and re-layouts: 6.51 us -> none  [fused(): wsend = jnp.stack([q_weight, k_weight, v_weight]).reshape(3, rows, 4, rows)]
    unnamed x10 -> x0, local copies, waits for them, and re-layouts: 3.35 us -> none
    transpose x1 -> x0, other arithmetic: 2.22 us -> none  [fused(): wsend = wsend.transpose(2, 0, 1, 3)]
    pallas_call x0 -> x1, Pallas kernels: none -> 1.82 us  [fused(): pl.pallas_call(place, out_shape=(jax.ShapeDtypeStruct(latent.shape, bf16)...]
    reshape x3 -> x0, local copies, waits for them, and re-layouts: 1.79 us -> none  [the longest x1 0.6 us: fused(): ln_gain.reshape(1, -1)]
where the time goes in v2:
time: 69.2 us; the launch traced here: 69.1 us
  Pallas kernels  65.8 us (95%)
  between operations  1.32 us (2%)
  other arithmetic  1.22 us (2%)
  local copies, waits for them, and re-layouts  0.73 us (1%)
    pallas_call x1, Pallas kernels, fused(): pl.pallas_call(kernel, out_shape=(jax.ShapeDtypeStruct(latent.shape, bf16...  64 us
    pallas_call x1, Pallas kernels, fused(): pl.pallas_call(place, out_shape=(jax.ShapeDtypeStruct(latent.shape, bf16)...  1.82 us

profile of v2, /device:TPU:0, one launch (start us, length us, event | category | flops | bytes accessed | tf_op | source)
XLA Modules:
  0.0 69.1 jit_solution(948589501001964660)
XLA Ops:
  1.3 1.0 %convert_reduce_fusion.1 = (f32[2]{0:T(128)S(1)}, f32[2]{0:T(128)S(1)}) fusion(s32[2,2]{1,0:T(2,128)} %param.18), kind=kLoop, calls=%fused_computation.6 | loop fusion | flops 4 | bytes 32 | tf_op jit(solution)/shard_map/convert_element_type | solution.py:43
  2.3 0.1 multiply_sine_fusion.2
  2.3 0.1 multiply_sine_fusion
  2.5 0.1 concatenate.3
  2.6 0.6 broadcast_in_dim.5.feats_ref
  3.3 64.0 %denoise.1 = (bf16[1,2,72,1280]{3,2,1,0:T(8,128)(2,1)}, bf16[1,2,72,512]{3,2,1,0:T(8,128)(2,1)}) custom-call(bf16[1,2,72,1280]{3,2,1,0:T(8,128)(2,1)} %latent_ref.1, bf16[1,2,72,512]{3,2,1,0:T(8,128)(2,1)} %dec_ref.1, bf16[16,960]{1,0:T(8,128)(2,1)} %broadcast_in_dim.5.feats_ref, f32[1280]{0:T(1024)} %gain_ref.1, f32[1280]{0:T(1024)} %shift_ref.1, ...), custom_call_target="tpu_custom_call" | custom-call | tf_op jit(solution)/shard_map/denoise/pallas_call | solution.py:672
  67.2 1.8 %place.1 = (bf16[1,2,72,1280]{3,2,1,0:T(8,128)(2,1)}, bf16[1,2,72,512]{3,2,1,0:T(8,128)(2,1)}) custom-call(bf16[1,2,72,1280]{3,2,1,0:T(8,128)(2,1)} %get-tuple-element.4.unet_ref, bf16[1,2,72,512]{3,2,1,0:T(8,128)(2,1)} %get-tuple-element.5.dec_ref), custom_call_target="tpu_custom_call" | custom-call | tf_op jit(solution)/shard_map/place/pallas_call | solution.py:737
  (4 shorter events, 0.1 us)

commit v3 on v2

--- a/solution.py
+++ b/solution.py
@@ -474,6 +474,16 @@
         where = spat.at[frame, :, pl.ds(pl.multiple_of(start, 128), size)]
         return remote(where, where, sp_send.at[n, k], sp_recv.at[n, k], k)
 
+    def entry(n):
+        return 1 if n == 1 else 2
+
+    def pass_on(n):
+        start, size = CHUNKS[n]
+        pf, pr = peer(entry(n))
+        spatial_copy(entry(n), n, pr, pf * share + start, size).wait_recv()
+        where = spat.at[pr, :, pl.ds(pl.multiple_of(pf * share + start, 128), size)]
+        remote(where, where, sp_send.at[n, 3], sp_recv.at[n, 3], 3 - entry(n)).start()
+
     for load in loads[1:4]:
         load.wait()
     for n, (start, size) in enumerate(CHUNKS):
@@ -489,13 +499,16 @@
         res = latbuf[:, :, :, column].astype(jnp.float32).reshape(2 * band, width, size)
         new = res + acc + cond[:, start : start + size].reshape(1, 1, size)
         spat[r, :, column] = new.reshape(2 * cells, size).astype(jnp.bfloat16)
-        for k in (3, 1, 2):
+        for k in (1, 2):
             spatial_copy(k, n, r, f * share + start, size).start()
         if n == 1:
             for k in (3, 1, 2):
                 weight_arrival(k).wait_recv()
                 weight_up(k, part).start()
                 weight_side(k, 0, part).start()
+
+    pass_on(0)
+    pass_on(1)
 
     dec_copy.wait_recv()
     for copy in stat_copies:
@@ -517,6 +530,8 @@
     dec_out_ref[0] = (
         (dec_values + temporal).reshape(band, width, dec_channels).astype(jnp.bfloat16)
     )
+
+    pass_on(2)
 
     head_size = channels // HEADS
     lane = lax.broadcasted_iota(jnp.int32, (rows, 128), 0)
@@ -528,7 +543,7 @@
         weight_up(k, part_above).wait_recv()
         weight_side(k, 1, part_above).start()
     for n, (start, size) in enumerate(CHUNKS):
-        for k in (1, 2, 3):
+        for k in (3 - entry(n), 3):
             pf, pr = peer(k)
             spatial_copy(k, n, pr, pf * share + start, size).wait_recv()
     for k in (3, 1, 2):
@@ -579,28 +594,45 @@
         mixed = jnp.concatenate(mixed, axis=0).astype(jnp.bfloat16)
         return jnp.dot(mixed, ow[...], preferred_element_type=jnp.float32)
 
-    def result_copy(k):
-        return remote(psend.at[k], precv.at[k], rs_send.at[k], rs_recv.at[k], k)
-
-    def tokens_of(frame):
-        return pl.ds(pl.multiple_of(frame * cells, 8), cells)
-
-    other = share_of(1 - r).astype(jnp.bfloat16)
+    middle_channel = channels // 2
+    left = slice(0, middle_channel)
+    right = slice(middle_channel, channels)
+
+    def result_copy(i):
+        slot, k, side = ((3, 1, 0), (3, 2, 1), (1, 1, 0), (1, 1, 1), (2, 2, 0), (2, 2, 1))[i]
+        columns = pl.ds(side * middle_channel, middle_channel)
+        return remote(
+            psend.at[slot, :, columns], precv.at[slot, :, columns], rs_send.at[i], rs_recv.at[i], k
+        )
+
+    other = share_of(1 - r)
     far = jnp.where(f == 0, other[cells:], other[:cells])
     near = jnp.where(f == 0, other[:cells], other[cells:])
-    psend[3] = far
+    psend[3] = far.astype(jnp.bfloat16)
+    result_copy(1).start()
+    result_copy(0).start()
+    psend[1, :, left] = near[:, left].astype(jnp.bfloat16)
+    result_copy(2).start()
+    own = share_of(r)
+    second = jnp.where(f == 0, own[cells:], own[:cells])
+    mine = jnp.where(f == 0, own[:cells], own[cells:])
+    psend[2, :, right] = second[:, right].astype(jnp.bfloat16)
+    result_copy(5).start()
+    result_copy(0).wait_recv()
+    psend[2, :, left] = (second[:, left] + precv[3, :, left].astype(jnp.float32)).astype(
+        jnp.bfloat16
+    )
+    result_copy(4).start()
+    result_copy(1).wait_recv()
+    psend[1, :, right] = (near[:, right] + precv[3, :, right].astype(jnp.float32)).astype(
+        jnp.bfloat16
+    )
     result_copy(3).start()
-    psend[1] = near
-    result_copy(1).start()
-    own = share_of(r)
-    psend[2] = jnp.where(f == 0, own[cells:], own[:cells]).astype(jnp.bfloat16)
-    result_copy(2).start()
-    mine = jnp.where(f == 0, own[:cells], own[cells:])
     where = pl.ds(pl.multiple_of(r * cells, 16), cells)
     result = spat[f, where, :].astype(jnp.float32) + mine
-    for k in (3, 1, 2):
-        result_copy(k).wait_recv()
-        result = result + precv[k].astype(jnp.float32)
+    for i in (2, 3, 4, 5):
+        result_copy(i).wait_recv()
+    result = result + precv[1].astype(jnp.float32) + precv[2].astype(jnp.float32)
     out_ref[0] = result.reshape(band, width, channels).astype(jnp.bfloat16)
 
     @pl.when(f == r)
@@ -618,12 +650,13 @@
     dec_copy.wait_send()
     for copy in stat_copies:
         copy.wait_send()
+    for i in range(6):
+        result_copy(i).wait_send()
     for k in (1, 2, 3):
         weight_copy(k).wait_send()
         weight_up(k, part).wait_send()
         weight_side(k, 0, part).wait_send()
         weight_side(k, 1, part_above).wait_send()
-        result_copy(k).wait_send()
         for n, (start, size) in enumerate(CHUNKS):
             spatial_copy(k, n, r, f * share + start, size).wait_send()
 
@@ -710,8 +743,8 @@
             dma((band,)),
             dma((3, 4)),
             dma((3, 4)),
-            dma((4,)),
-            dma((4,)),
+            dma((6,)),
+            dma((6,)),
         ],
         compiler_params=pltpu.CompilerParams(
             collective_id=0, has_side_effects=True, vmem_limit_bytes=60 * 1024 * 1024

time: 69.2 us -> 64.2 us (0.928)
  Pallas kernels: 65.8 us -> 60.8 us
    pallas_call x1, Pallas kernels: 64 us -> 59 us  [fused(): pl.pallas_call(kernel, out_shape=(jax.ShapeDtypeStruct(latent.shape, bf16...]
where the time goes in v3:
time: 64.2 us; the launch traced here: 64.1 us
  Pallas kernels  60.8 us (95%)
  between operations  1.32 us (2%)
  other arithmetic  1.22 us (2%)
  local copies, waits for them, and re-layouts  0.73 us (1%)
    pallas_call x1, Pallas kernels, fused(): pl.pallas_call(kernel, out_shape=(jax.ShapeDtypeStruct(latent.shape, bf16...  59 us
    pallas_call x1, Pallas kernels, fused(): pl.pallas_call(place, out_shape=(jax.ShapeDtypeStruct(latent.shape, bf16)...  1.82 us

profile of v3, /device:TPU:0, one launch (start us, length us, event | category | flops | bytes accessed | tf_op | source)
XLA Modules:
  0.0 64.1 jit_solution(6043077406842660180)
XLA Ops:
  1.3 1.0 %convert_reduce_fusion.1 = (f32[2]{0:T(128)S(1)}, f32[2]{0:T(128)S(1)}) fusion(s32[2,2]{1,0:T(2,128)} %param.18), kind=kLoop, calls=%fused_computation.6 | loop fusion | flops 4 | bytes 32 | tf_op jit(solution)/shard_map/convert_element_type | solution.py:43
  2.3 0.1 multiply_sine_fusion.2
  2.3 0.1 multiply_sine_fusion
  2.5 0.1 concatenate.3
  2.6 0.6 broadcast_in_dim.5.feats_ref
  3.3 59.0 %denoise.1 = (bf16[1,2,72,1280]{3,2,1,0:T(8,128)(2,1)}, bf16[1,2,72,512]{3,2,1,0:T(8,128)(2,1)}) custom-call(bf16[1,2,72,1280]{3,2,1,0:T(8,128)(2,1)} %latent_ref.1, bf16[1,2,72,512]{3,2,1,0:T(8,128)(2,1)} %dec_ref.1, bf16[16,960]{1,0:T(8,128)(2,1)} %broadcast_in_dim.5.feats_ref, f32[1280]{0:T(1024)} %gain_ref.1, f32[1280]{0:T(1024)} %shift_ref.1, ...), custom_call_target="tpu_custom_call" | custom-call | tf_op jit(solution)/shard_map/denoise/pallas_call | solution.py:705
  62.2 1.8 %place.1 = (bf16[1,2,72,1280]{3,2,1,0:T(8,128)(2,1)}, bf16[1,2,72,512]{3,2,1,0:T(8,128)(2,1)}) custom-call(bf16[1,2,72,1280]{3,2,1,0:T(8,128)(2,1)} %get-tuple-element.4.unet_ref, bf16[1,2,72,512]{3,2,1,0:T(8,128)(2,1)} %get-tuple-element.5.dec_ref), custom_call_target="tpu_custom_call" | custom-call | tf_op jit(solution)/shard_map/place/pallas_call | solution.py:770
  (4 shorter events, 0.1 us)

commit v4 on v3

--- a/solution.py
+++ b/solution.py
@@ -235,7 +235,8 @@
 def kernel(
     latent_ref,
     dec_ref,
-    feats_ref,
+    time_ref,
+    camera_ref,
     gain_ref,
     shift_ref,
     ln_ref,
@@ -394,8 +395,27 @@
     )
     local_weight.start()
 
+    entries = emb.shape[0] // 3
+    lanes = lax.broadcasted_iota(jnp.int32, (8, 3 * entries), 1)
+    second_piece = lanes >= entries
+    third_piece = lanes >= 2 * entries
+    entry_at = jnp.where(
+        third_piece, lanes - 2 * entries, jnp.where(second_piece, lanes - entries, lanes)
+    )
+    is_sine = entry_at >= entries // 2
+    order = jnp.where(is_sine, entry_at - entries // 2, entry_at).astype(jnp.float32)
+    freqs = jnp.exp(-math.log(10000.0) * order / (entries // 2))
+    value = jnp.where(
+        third_piece,
+        camera_ref[r, 1].astype(jnp.float32),
+        jnp.where(
+            second_piece, camera_ref[r, 0].astype(jnp.float32), time_ref[0].astype(jnp.float32)
+        ),
+    )
+    angles = value * freqs
+    feats = silu(jnp.where(is_sine, jnp.sin(angles), jnp.cos(angles))).astype(jnp.bfloat16)
     loads[0].wait()
-    cond = jnp.dot(feats_ref[...], emb[...], preferred_element_type=jnp.float32)[0:1]
+    cond = jnp.dot(feats, emb[...], preferred_element_type=jnp.float32)[0:1]
 
     xcat[0:stride, :] = jnp.zeros((stride, 3 * channels), jnp.bfloat16)
     xcat[5 * stride : 6 * stride, :] = jnp.zeros((stride, 3 * channels), jnp.bfloat16)
@@ -695,10 +715,8 @@
     rows = q_weight.shape[0]
     cells = band * width
     dec_channels = dec_feat.shape[3]
-    features = conditions(timestep, camera, 2, emb_weight.shape[0] // 3)
-    feats = lax.dynamic_slice_in_dim(features, lax.axis_index("row"), 1, 0)
-    feats = jnp.broadcast_to(feats, (16, feats.shape[1]))
     vmem = pl.BlockSpec(memory_space=pltpu.VMEM)
+    smem = pl.BlockSpec(memory_space=pltpu.SMEM)
     hbm = pl.BlockSpec(memory_space=pl.ANY)
     dma = pltpu.SemaphoreType.DMA
     bf16, f32 = jnp.bfloat16, jnp.float32
@@ -708,7 +726,7 @@
             jax.ShapeDtypeStruct(latent.shape, bf16),
             jax.ShapeDtypeStruct(dec_feat.shape, bf16),
         ),
-        in_specs=[vmem] * 8 + [hbm] * 7,
+        in_specs=[vmem] * 2 + [smem] * 2 + [vmem] * 5 + [hbm] * 7,
         out_specs=(vmem, vmem),
         scratch_shapes=[
             pltpu.VMEM((3, rows, channels), bf16),
@@ -753,7 +771,8 @@
     )(
         latent,
         dec_feat,
-        feats,
+        timestep,
+        camera,
         norm_gain,
         norm_shift,
         ln_gain,

time: 64.2 us -> 62.3 us (0.970)
  other arithmetic: 1.22 us -> 0 us
  local copies, waits for them, and re-layouts: 0.73 us -> 0 us
    convert_element_type x1 -> x0, other arithmetic: 0.97 us -> none  [sinusoids(): angles = values.astype(jnp.float32)[..., None] * freqs]
where the time goes in v4:
time: 62.3 us; the launch traced here: 62.2 us
  Pallas kernels  60.9 us (98%)
  between operations  1.29 us (2%)
    pallas_call x1, Pallas kernels, fused(): pl.pallas_call(kernel, out_shape=(jax.ShapeDtypeStruct(latent.shape, bf16...  59.1 us
    pallas_call x1, Pallas kernels, fused(): pl.pallas_call(place, out_shape=(jax.ShapeDtypeStruct(latent.shape, bf16)...  1.82 us

profile of v4, /device:TPU:0, one launch (start us, length us, event | category | flops | bytes accessed | tf_op | source)
XLA Modules:
  0.0 62.2 jit_solution(16646496467357407517)
XLA Ops:
  1.3 59.1 %denoise.1 = (bf16[1,2,72,1280]{3,2,1,0:T(8,128)(2,1)}, bf16[1,2,72,512]{3,2,1,0:T(8,128)(2,1)}) custom-call(bf16[1,2,72,1280]{3,2,1,0:T(8,128)(2,1)} %latent_ref.1, bf16[1,2,72,512]{3,2,1,0:T(8,128)(2,1)} %dec_ref.1, s32[1]{0:T(128)S(6)} %copy.18.time_ref, s32[2,2]{1,0:T(2,128)} %camera_ref.1, f32[1280]{0:T(1024)} %gain_ref.1, f32[1280]{0:T(1024)} %shift_ref.1, ...), custom_call_target="tpu_custom_call" | custom-call | tf_op jit(solution)/shard_map/denoise/pallas_call | solution.py:723
  60.3 1.8 %place.1 = (bf16[1,2,72,1280]{3,2,1,0:T(8,128)(2,1)}, bf16[1,2,72,512]{3,2,1,0:T(8,128)(2,1)}) custom-call(bf16[1,2,72,1280]{3,2,1,0:T(8,128)(2,1)} %get-tuple-element.4.unet_ref, bf16[1,2,72,512]{3,2,1,0:T(8,128)(2,1)} %get-tuple-element.5.dec_ref), custom_call_target="tpu_custom_call" | custom-call | tf_op jit(solution)/shard_map/place/pallas_call | solution.py:789
